TPU v7x, 32 devices: a whole 2x2x4 slice. The times are simulated.
32 devices in a mesh: groups: 2 (over x), items: 16 (over z, y, core).
Axes of the slice: x: 2, y: 2, z: 4, core: 2. Of those that a mesh axis runs over, the one named last changes fastest.
Arguments:
- candidate_traits: bfloat16 [16384, 2048], P(('groups', 'items')), parts along dimension 0, may hold values from -6 to 6
- candidate_tower_matrix: bfloat16 [2048, 512], replicated, may hold values from -0.125 to 0.125
- query_vectors: bfloat16 [128, 512], P(('groups', 'items')), parts along dimension 0, may hold values from -6 to 6
- kept_positions: int32 [128, 128], P('groups', 'items'), parts along dimension 0, may hold values from 0 to 511
- ranker_first_matrix: bfloat16 [1024, 1024], replicated, may hold values from -0.1875 to 0.1875
- ranker_second_matrix: bfloat16 [1024, 1024], replicated, may hold values from -0.1875 to 0.1875
- ranker_final_vector: bfloat16 [1024], replicated, may hold values from -0.1875 to 0.1875
Outputs:
- prescore: float32 [16384, 64], P(('groups', 'items')), parts along dimension 0
- ranking: float32 [128, 128], P(('groups', 'items')), parts along dimension 0
There are 2 independent parts, one for each index of `groups`. A program takes and returns all parts, laid end to end along the dimension named above; an argument that names none is the same for every part. Nothing has to cross between parts.
Inputs may be any that keep to these rules, and one draw needn't show every extreme that they name: `kept_positions`: entry j of a request is a position within item shard j // 8, which holds items j // 8 * 512 onward.
All inputs are finite; a program needn't handle non-finite values.
Results may differ from a plain program's by a relative error of at most 0.013.
Values may be sent and summed in bfloat16 or wider, within the bound.
A program may use at most 64 MiB of HBM per device.

v0:
```python
import jax
import jax.numpy as jnp
from jax import lax
from jax.sharding import PartitionSpec as P


def item_tower(candidate_traits, candidate_tower_matrix):
    raw = jnp.dot(candidate_traits, candidate_tower_matrix, preferred_element_type=jnp.float32)
    factor = lax.rsqrt(jnp.mean(raw * raw, axis=-1, keepdims=True) + 1e-06)
    return (raw * factor).astype(jnp.bfloat16)


def cross_tower(
    item_rows, user_rows, ranker_first_matrix, ranker_second_matrix, ranker_final_vector
):
    owned, count, width = item_rows.shape
    product = (item_rows.astype(jnp.float32) * user_rows.astype(jnp.float32)[:, None, :]).astype(
        jnp.bfloat16
    )
    cross_in = jnp.concatenate([product, item_rows], axis=-1).reshape(owned * count, 2 * width)
    hidden_one = jax.nn.silu(
        jnp.dot(cross_in, ranker_first_matrix, preferred_element_type=jnp.float32)
    ).astype(jnp.bfloat16)
    hidden_two = jax.nn.silu(
        jnp.dot(hidden_one, ranker_second_matrix, preferred_element_type=jnp.float32)
    ).astype(jnp.bfloat16)
    return jnp.dot(hidden_two, ranker_final_vector, preferred_element_type=jnp.float32).reshape(
        owned, count
    )


def per_device(
    candidate_traits,
    candidate_tower_matrix,
    query_vectors,
    kept_positions,
    ranker_first_matrix,
    ranker_second_matrix,
    ranker_final_vector,
):
    candidate_vectors = item_tower(candidate_traits, candidate_tower_matrix)
    width = candidate_vectors.shape[1]
    all_users = lax.all_gather(query_vectors, "items", axis=0, tiled=True)
    prescore = lax.dot_general(
        candidate_vectors, all_users, (((1,), (1,)), ((), ())), preferred_element_type=jnp.float32
    ) * width ** (-0.5)
    selected_candidates = jnp.take(candidate_vectors, kept_positions, axis=0)
    item_rows = lax.all_to_all(
        selected_candidates, "items", split_axis=0, concat_axis=1, tiled=True
    )
    ranking = cross_tower(
        item_rows, query_vectors, ranker_first_matrix, ranker_second_matrix, ranker_final_vector
    )
    return (prescore, ranking)


def solution(mesh):
    placed = (
        P(("groups", "items"), None),
        P(),
        P(("groups", "items"), None),
        P("groups", "items"),
        P(),
        P(),
        P(),
    )
    return jax.shard_map(
        per_device,
        mesh=mesh,
        in_specs=placed,
        out_specs=(P(("groups", "items"), None), P(("groups", "items"), None)),
        check_vma=False,
    )
```

profile of v0, /device:TPU:0, one launch (start us, length us, event | category | flops | bytes accessed | tf_op | source)
XLA Modules:
  0.0 51.8 jit_solution(16912730754630676367)
XLA Ops:
  0.6 0.0 copy-start
  0.6 0.8 %compare_and_fusion = pred[64,8]{0,1:T(8,128)(4,1)S(1)} fusion(s32[64,8]{0,1:T(8,128)} %param.10), kind=kLoop, calls=%fused_computation.18 | loop fusion | flops 3072 | bytes 2560 | tf_op jit(solution)/shard_map/jit(_take)/and | solution.py:47
  1.5 0.7 %compare_select_fusion = s32[64,8]{0,1:T(8,128)S(1)} fusion(s32[64,8]{0,1:T(8,128)} %param.10), kind=kLoop, calls=%fused_computation.16 | loop fusion | flops 1536 | bytes 4096 | tf_op jit(solution)/shard_map/jit(_take)/jit(_where)/select_n | solution.py:47
  2.2 0.1 copy.18
  2.3 0.1 copy.19
  2.4 0.1 reshape.30
  2.5 3.5 %multiply_reduce_fusion = (f32[512]{0:T(512)S(1)}, f32[512,512]{0,1:T(8,128)S(1)}) fusion(bf16[512,2048]{1,0:T(8,128)(2,1)} %param.7, bf16[2048,512]{1,0:T(8,128)(2,1)} %param.8), kind=kOutput, calls=%fused_computation.14 | convolution fusion | flops 1074265600 | bytes 5244928 | tf_op jit(solution)/shard_map/dot_general | solution.py:8
  6.0 0.1 multiply_convert_fusion.7
  6.1 0.2 copy.20
  6.4 2.6 %gather_fusion = bf16[512,512]{1,0:T(8,128)(2,1)} fusion(bf16[512,512]{1,0:T(8,128)(2,1)S(1)} %copy.20, s32[1024]{0:T(1024)S(1)} %pad_clamp_fusion), kind=kCustom, calls=%fused_computation | custom fusion | bytes 1050624 | tf_op jit(solution)/shard_map/jit(_take)/gather | solution.py:47
  9.0 0.0 copy-start.2
  9.0 0.0 copy-start.1
  9.0 2.0 %bitcast_select_fusion = bf16[64,8,512]{2,1,0:T(8,128)(2,1)} fusion(bf16[512,512]{1,0:T(8,128)(2,1)} %gather_fusion, pred[64,8]{1,0:T(8,128)(4,1)S(1)} %copy.18), kind=kLoop, calls=%fused_computation.15 | loop fusion | flops 262144 | bytes 1049088 | tf_op jit(solution)/shard_map/jit(_take)/select_n | solution.py:47
  11.0 7.4 %all-to-all-start = ((bf16[64,8,512]{2,1,0:T(8,128)(2,1)}), bf16[64,8,512]{2,1,0:T(8,128)(2,1)S(1)}, u32[]{:S(2)}, u32[]{:S(2)}) async-start(bf16[64,8,512]{2,1,0:T(8,128)(2,1)} %bitcast_select_fusion), calls=%async_computation | async-start | bytes 1048576 | tf_op jit(solution)/shard_map/all_to_all | solution.py:48
  18.4 0.0 copy-done.2
  18.4 0.0 copy-done.1
  18.4 25.1 %all-gather = bf16[16,4,512]{2,1,0:T(4,128)(2,1)S(1)} all-gather(bf16[1,4,512]{2,1,0:T(4,128)(2,1)S(1)} %bitcast.24), channel_id=1, replica_groups=mesh['groups'=2,'items'=16] {'items'}, dimensions={0}, use_global_device_ids=true | all-gather | bytes 69632 | tf_op jit(solution)/shard_map/all_gather | solution.py:43
  43.6 0.9 %convolution_multiply_fusion = f32[512,64]{0,1:T(8,128)} fusion(bf16[64,512]{1,0:T(8,128)(2,1)S(1)} %reshape.39, bf16[512,512]{0,1:T(8,128)(2,1)S(1)} %multiply_convert_fusion.7), kind=kOutput, calls=%fused_computation.3 | convolution fusion | flops 33587200 | bytes 720896 | tf_op jit(solution)/shard_map/dot_general | solution.py:44
  44.4 0.0 all-to-all-done
  44.5 0.1 fusion.6
  44.6 0.0 copy-done
  44.6 2.6 %fusion.2 = f32[512,1024]{1,0:T(8,128)} fusion(bf16[1024,1024]{1,0:T(8,128)(2,1)S(1)} %copy-done, bf16[512,512]{1,0:T(8,128)(2,1)S(1)} %bitcast.23, bf16[512,512]{1,0:T(8,128)(2,1)S(1)} %fusion.6), kind=kOutput, calls=%fused_computation.6 | convolution fusion | flops 1075838976 | bytes 5242880 | tf_op jit(solution)/shard_map/dot_general | solution.py:22
  47.2 4.6 %fusion.1 = f32[1,512]{1,0:T(1,128)} fusion(bf16[1024,1]{0,1:T(2,128)(2,1)S(1)} %reshape.40, bf16[1024,1024]{1,0:T(8,128)(2,1)} %param.12, f32[512,1024]{1,0:T(8,128)} %fusion.2), kind=kOutput, calls=%fused_computation.5 | convolution fusion | flops 1080033280 | bytes 4198400 | tf_op jit(solution)/shard_map/dot_general | solution.py:27
  (6 shorter events, 0.1 us)
Async XLA Ops:
  0.6 44.0 %copy-start = (bf16[1024,1024]{1,0:T(8,128)(2,1)S(1)}, bf16[1024,1024]{1,0:T(8,128)(2,1)}, u32[]{:S(2)}) copy-start(bf16[1024,1024]{1,0:T(8,128)(2,1)} %param.11) | copy-start | bytes 6291460
  9.0 9.4 %copy-start.2 = (bf16[1024]{0:T(1024)(128)(2,1)S(1)}, bf16[1024]{0:T(1024)(128)(2,1)}, u32[]{:S(2)}) copy-start(bf16[1024]{0:T(1024)(128)(2,1)} %param.13) | copy-start | bytes 6148
  9.0 9.4 %copy-start.1 = (bf16[4,512]{1,0:T(4,128)(2,1)S(1)}, bf16[4,512]{1,0:T(4,128)(2,1)}, u32[]{:S(2)}) copy-start(bf16[4,512]{1,0:T(4,128)(2,1)} %param.9) | copy-start | bytes 12292
  11.0 33.5 %all-to-all-start = ((bf16[64,8,512]{2,1,0:T(8,128)(2,1)}), bf16[64,8,512]{2,1,0:T(8,128)(2,1)S(1)}, u32[]{:S(2)}, u32[]{:S(2)}) async-start(bf16[64,8,512]{2,1,0:T(8,128)(2,1)} %bitcast_select_fusion), calls=%async_computation | async-start | bytes 1048576 | tf_op jit(solution)/shard_map/all_to_all | solution.py:48
where the time goes:
time: 52.1 us; the launch traced here: 51.8 us
  blocking collectives  25.1 us (48%)
  matrix products  11.6 us (22%)
  starting transfers between devices  7.41 us (14%)
  other arithmetic  3.79 us (7%)
  local copies, waits for them, and re-layouts  3.19 us (6%)
  between operations  0.73 us (1%)
    all_gather x1, blocking collectives, per_device(): all_users = lax.all_gather(query_vectors, 'items', axis=0, tiled=True)  25.1 us
    all_to_all x1, starting transfers between devices, per_device(): lax.all_to_all(selected_candidates, 'items', split_axis=0, concat_axis=1,...  7.41 us
    dot_general x1, matrix products, cross_tower(): jnp.dot(hidden_two, ranker_final_vector, preferred_element_type=jnp.float32)  4.56 us
    dot_general x1, matrix products, item_tower(): jnp.dot(candidate_traits, candidate_tower_matrix, preferred_element_type=...  3.53 us
    select_n x2, other arithmetic, per_device(): selected_candidates = jnp.take(candidate_vectors, kept_positions, axis=0)  2.68 us
    dot_general x1, matrix products, cross_tower(): jnp.dot(cross_in, ranker_first_matrix, preferred_element_type=jnp.float32)  2.63 us
    gather x1, local copies, waits for them, and re-layouts, per_device(): selected_candidates = jnp.take(candidate_vectors, kept_positions, axis=0)  2.61 us
  transfers between devices with their start and end apart: 1, of which 0 were waited for; matrix products, arithmetic and copies ran while one was open for 2% of the time, Pallas kernels for 0%

commit v1 on v0

v1 whole, which is shorter than its diff:
```python
import functools

import jax
import jax.numpy as jnp
from jax import lax
from jax.experimental import pallas as pl
from jax.experimental.pallas import tpu as pltpu
from jax.sharding import PartitionSpec as P

LANES = 128
F32 = jnp.float32
BF16 = jnp.bfloat16


def silu(v):
    half = 0.5 * v
    return half + half * jnp.tanh(half)


def nt_dot(a, b):
    return lax.dot_general(a, b, (((1,), (1,)), ((), ())), preferred_element_type=F32)


def cascade(
    n,
    cuts,
    greet_after,
    traits,
    tower,
    query,
    kept,
    first,
    second,
    final,
    prescore,
    ranking,
    traits_v,
    tower_v,
    first_v,
    second_v,
    final_v,
    kept_v,
    users_in,
    users_f,
    embedded,
    raw,
    pre_v,
    part,
    sends,
    parts_in,
    rank_v,
    in_sems,
    load_sems,
    out_sems,
    user_send,
    user_recv,
    part_send,
    part_recv,
):
    me = lax.axis_index("items")
    owned = query.shape[0]
    requests = n * owned
    width = embedded.shape[1]
    catalog = embedded.shape[0]
    depth = tower.shape[0]
    per_shard = kept.shape[0]
    hidden = first.shape[1]

    barrier = pltpu.get_barrier_semaphore()
    for k in range(1, n):
        pl.semaphore_signal(
            barrier,
            inc=1,
            device_id={"items": lax.rem(me + k, n)},
            device_id_type=pl.DeviceIdType.MESH,
        )

    step = depth // cuts
    tower_loads = []
    for c in range(cuts):
        at = pl.ds(c * step, step)
        pair = (
            pltpu.make_async_copy(tower.at[at, :], tower_v.at[at, :], in_sems.at[2 * c]),
            pltpu.make_async_copy(traits.at[:, at], traits_v.at[:, at], in_sems.at[2 * c + 1]),
        )
        for load in pair:
            load.start()
        tower_loads.append(pair)
    own_users = pltpu.make_async_copy(query, users_in.at[me], load_sems.at[0])
    kept_load = pltpu.make_async_copy(kept, kept_v, load_sems.at[1])
    first_load = pltpu.make_async_copy(first, first_v, load_sems.at[2])
    second_load = pltpu.make_async_copy(second, second_v, load_sems.at[3])
    final_load = pltpu.make_async_copy(final, final_v, load_sems.at[4])
    for load in (own_users, kept_load, first_load, second_load, final_load):
        load.start()

    def user_copy(k):
        return pltpu.make_async_remote_copy(
            src_ref=query,
            dst_ref=users_in.at[me],
            send_sem=user_send.at[k],
            recv_sem=user_recv.at[me],
            device_id={"items": lax.rem(me + k, n)},
            device_id_type=pl.DeviceIdType.MESH,
        )

    def user_arrival(k):
        source = lax.rem(me + n - k, n)
        return pltpu.make_async_remote_copy(
            src_ref=query,
            dst_ref=users_in.at[source],
            send_sem=user_send.at[k],
            recv_sem=user_recv.at[source],
            device_id={"items": lax.rem(me + k, n)},
            device_id_type=pl.DeviceIdType.MESH,
        )

    for c in range(cuts):
        if c == greet_after:
            pl.semaphore_wait(barrier, n - 1)
            for k in range(1, n):
                user_copy(k).start()
        for load in tower_loads[c]:
            load.wait()
        at = pl.ds(c * step, step)
        term = jnp.dot(traits_v[:, at], tower_v[at, :], preferred_element_type=F32)
        if c == 0:
            raw[...] = term
        else:
            raw[...] += term
    total = raw[...]
    factor = lax.rsqrt(jnp.mean(total * total, axis=-1, keepdims=True) + 1e-06)
    embedded[...] = (total * factor).astype(BF16)

    kept_load.wait()
    columns = kept_v[...].T
    block = min(requests, 64)
    places = lax.broadcasted_iota(jnp.int32, (block, catalog), 1)
    lane = lax.broadcasted_iota(jnp.int32, (block, LANES), 1)
    shards_per_tile = LANES // per_shard
    home = lax.rem(me, shards_per_tile) * per_shard
    final_load.wait()
    final_rows = final_v[...].astype(F32)
    final_row = jnp.concatenate(
        [final_rows[i : i + 1, :] for i in range(hidden // LANES)], axis=1
    )
    final_wide = jnp.broadcast_to(final_row, (LANES, hidden)).astype(BF16)

    for b in range(requests // block):
        rows = slice(b * block, (b + 1) * block)
        pick = jnp.concatenate(
            [
                jnp.where(columns[rows, j : j + 1] == places, 1.0, 0.0).astype(BF16)
                for j in range(per_shard)
            ],
            axis=0,
        )
        chosen = jnp.dot(pick, embedded[...], preferred_element_type=F32).astype(BF16)
        if b == 0:
            first_load.wait()
        pre_one = jnp.dot(chosen, first_v[width:, :], preferred_element_type=F32)
        if b == 0:
            own_users.wait()
            for k in range(1, n):
                user_arrival(k).wait_recv()
            for i in range(n):
                users_f[i * owned : (i + 1) * owned, :] = users_in[i].astype(F32)
        users = users_f[rows, :].astype(BF16)
        product = chosen * jnp.concatenate([users] * per_shard, axis=0)
        pre_one += jnp.dot(product, first_v[:width, :], preferred_element_type=F32)
        hidden_one = silu(pre_one).astype(BF16)
        if b == 0:
            second_load.wait()
        hidden_two = silu(
            jnp.dot(hidden_one, second_v[...], preferred_element_type=F32)
        ).astype(BF16)
        scores = nt_dot(hidden_two, final_wide)
        mine = jnp.zeros((block, LANES), F32)
        for j in range(per_shard):
            mine = jnp.where(
                lane == home + j, scores[j * block : (j + 1) * block, :], mine
            )
        part[rows, :] = mine
    for i in range(n):
        sends[i] = part[i * owned : (i + 1) * owned, :]

    def part_copy(k):
        peer = lax.rem(me + k, n)
        return pltpu.make_async_remote_copy(
            src_ref=sends.at[peer],
            dst_ref=parts_in.at[me],
            send_sem=part_send.at[k],
            recv_sem=part_recv.at[me],
            device_id={"items": peer},
            device_id_type=pl.DeviceIdType.MESH,
        )

    def part_arrival(k):
        source = lax.rem(me + n - k, n)
        return pltpu.make_async_remote_copy(
            src_ref=sends.at[source],
            dst_ref=parts_in.at[source],
            send_sem=part_send.at[k],
            recv_sem=part_recv.at[source],
            device_id={"items": source},
            device_id_type=pl.DeviceIdType.MESH,
        )

    for k in range(1, n):
        part_copy(k).start()

    pre_v[...] = nt_dot(users_f[...].astype(BF16), embedded[...]) * width ** (-0.5)
    pre_out = pltpu.make_async_copy(pre_v, prescore, out_sems.at[0])
    pre_out.start()

    parts_in[me] = sends[me]
    for k in range(1, n):
        part_arrival(k).wait_recv()
    for t in range(n // shards_per_tile):
        total = parts_in[t * shards_per_tile]
        for s in range(t * shards_per_tile + 1, (t + 1) * shards_per_tile):
            total = total + parts_in[s]
        rank_v[:, t * LANES : (t + 1) * LANES] = total
    rank_out = pltpu.make_async_copy(rank_v, ranking, out_sems.at[1])
    rank_out.start()
    for k in range(1, n):
        user_copy(k).wait_send()
        part_copy(k).wait_send()
    pre_out.wait()
    rank_out.wait()


def per_device(
    n,
    candidate_traits,
    candidate_tower_matrix,
    query_vectors,
    kept_positions,
    ranker_first_matrix,
    ranker_second_matrix,
    ranker_final_vector,
):
    catalog, depth = candidate_traits.shape
    width = candidate_tower_matrix.shape[1]
    owned = query_vectors.shape[0]
    requests, per_shard = kept_positions.shape
    hidden = ranker_first_matrix.shape[1]
    cuts = 4
    anywhere = pl.BlockSpec(memory_space=pl.ANY)
    prescore, ranking = pl.pallas_call(
        functools.partial(cascade, n, cuts, 2),
        out_shape=(
            jax.ShapeDtypeStruct((requests, catalog), F32),
            jax.ShapeDtypeStruct((owned, n * per_shard), F32),
        ),
        in_specs=[anywhere] * 7,
        out_specs=(anywhere, anywhere),
        scratch_shapes=[
            pltpu.VMEM((catalog, depth), BF16),
            pltpu.VMEM((depth, width), BF16),
            pltpu.VMEM(ranker_first_matrix.shape, BF16),
            pltpu.VMEM(ranker_second_matrix.shape, BF16),
            pltpu.VMEM((hidden // LANES, LANES), BF16),
            pltpu.VMEM((per_shard, requests), jnp.int32),
            pltpu.VMEM((n, owned, width), BF16),
            pltpu.VMEM((requests, width), F32),
            pltpu.VMEM((catalog, width), BF16),
            pltpu.VMEM((catalog, width), F32),
            pltpu.VMEM((requests, catalog), F32),
            pltpu.VMEM((requests, LANES), F32),
            pltpu.VMEM((n, owned, LANES), F32),
            pltpu.VMEM((n, owned, LANES), F32),
            pltpu.VMEM((owned, n * per_shard), F32),
            pltpu.SemaphoreType.DMA((2 * cuts,)),
            pltpu.SemaphoreType.DMA((5,)),
            pltpu.SemaphoreType.DMA((2,)),
            pltpu.SemaphoreType.DMA((n,)),
            pltpu.SemaphoreType.DMA((n,)),
            pltpu.SemaphoreType.DMA((n,)),
            pltpu.SemaphoreType.DMA((n,)),
        ],
        compiler_params=pltpu.CompilerParams(collective_id=0, has_side_effects=True),
        name="cascade",
    )(
        candidate_traits,
        candidate_tower_matrix,
        query_vectors,
        kept_positions.T,
        ranker_first_matrix,
        ranker_second_matrix,
        ranker_final_vector.reshape(hidden // LANES, LANES),
    )
    return (prescore.T, ranking)


def solution(mesh):
    placed = (
        P(("groups", "items"), None),
        P(),
        P(("groups", "items"), None),
        P("groups", "items"),
        P(),
        P(),
        P(),
    )
    return jax.shard_map(
        functools.partial(per_device, mesh.shape["items"]),
        mesh=mesh,
        in_specs=placed,
        out_specs=(P(("groups", "items"), None), P(("groups", "items"), None)),
        check_vma=False,
    )
```

time: 52.1 us -> 22.9 us (0.44)
  blocking collectives: 25.1 us -> 0 us
  Pallas kernels: 0 us -> 19.3 us
  matrix products: 11.6 us -> 0 us
  starting transfers between devices: 7.41 us -> 0 us
  other arithmetic: 3.79 us -> 0 us
    all_gather x1 -> x0, blocking collectives: 25.1 us -> none  [per_device(): all_users = lax.all_gather(query_vectors, 'items', axis=0, tiled=True)]
    pallas_call x0 -> x1, Pallas kernels: none -> 19.3 us  [per_device(): pl.pallas_call(functools.partial(cascade, n, cuts, 2), out_shape=(jax.Sha...]
    dot_general x4 -> x0, matrix products: 11.6 us -> none  [the longest x1 4.56 us: cross_tower(): jnp.dot(hidden_two, ranker_final_vector, preferred_element_type=jnp.float32)]
    all_to_all x1 -> x0, starting transfers between devices: 7.41 us -> none  [per_device(): lax.all_to_all(selected_candidates, 'items', split_axis=0, concat_axis=1,...]
    unnamed x8 -> x2, local copies, waits for them, and re-layouts: 0.04 us -> 2.83 us
    select_n x2 -> x0, other arithmetic: 2.68 us -> none  [per_device(): selected_candidates = jnp.take(candidate_vectors, kept_positions, axis=0)]
    gather x1 -> x0, local copies, waits for them, and re-layouts: 2.61 us -> none  [per_device(): selected_candidates = jnp.take(candidate_vectors, kept_positions, axis=0)]
    and x1 -> x0, other arithmetic: 0.84 us -> none  [per_device(): selected_candidates = jnp.take(candidate_vectors, kept_positions, axis=0)]
  transfers between devices with their start and end apart: 1 -> 0, of which waited for: 0 -> 0; matrix products, arithmetic and copies ran while one was open for 2% -> 0% of each run, Pallas kernels for 0% -> 0%
where the time goes in v1:
time: 22.9 us; the launch traced here: 22.8 us
  Pallas kernels  19.3 us (84%)
  local copies, waits for them, and re-layouts  2.83 us (12%)
  between operations  0.64 us (3%)
    pallas_call x1, Pallas kernels, per_device(): pl.pallas_call(functools.partial(cascade, n, cuts, 2), out_shape=(jax.Sha...  19.3 us
    unnamed x2, local copies, waits for them, and re-layouts  2.83 us

profile of v1, /device:TPU:0, one launch (start us, length us, event | category | flops | bytes accessed | tf_op | source)
XLA Modules:
  0.0 22.8 jit_solution(14983283046166395354)
XLA Ops:
  0.6 19.3 %cascade.1 = (f32[64,512]{1,0:T(8,128)}, f32[4,128]{1,0:T(4,128)}) custom-call(bf16[512,2048]{1,0:T(8,128)(2,1)} %traits.1, bf16[2048,512]{1,0:T(8,128)(2,1)} %tower.1, bf16[4,512]{1,0:T(4,128)(2,1)} %query.1, s32[8,64]{1,0:T(8,128)} %bitcast.4, bf16[1024,1024]{1,0:T(8,128)(2,1)} %first.1, bf16[1024,1024]{1,0:T(8,128)(2,1)} %second.1, bf16[8,128]{1,0:T(8,128)(2,1)} %bitcast.5), custom_call_target="tpu_custom_call" | custom-call | tf_op jit(solution)/shard_map/cascade/pallas_call | solution.py:250
  19.9 1.6 %copy.11 = f32[512,64]{0,1:T(8,128)} copy(f32[512,64]{0,1:T(8,128)} %bitcast.3) | data formatting | bytes 262144
  21.5 1.3 %copy.12 = f32[4,128]{1,0:T(4,128)} copy(f32[4,128]{1,0:T(4,128)} %get-tuple-element.9) | data formatting | bytes 4096

commit v2 on v1

v2 whole, which is shorter than its diff:
```python
import functools

import jax
import jax.numpy as jnp
from jax import lax
from jax.experimental import pallas as pl
from jax.experimental.pallas import tpu as pltpu
from jax.sharding import PartitionSpec as P

LANES = 128
TILE = 256
CUTS = 4
GREET_AFTER = 1
F32 = jnp.float32
BF16 = jnp.bfloat16


def silu(v):
    half = 0.5 * v
    return half + half * jnp.tanh(half)


def nt_dot(a, b):
    return lax.dot_general(a, b, (((1,), (1,)), ((), ())), preferred_element_type=F32)


def cascade(
    n,
    traits,
    tower,
    query,
    kept,
    first,
    second,
    final,
    pre_v,
    rank_v,
    traits_v,
    tower_v,
    first_v,
    second_v,
    final_v,
    kept_v,
    users_in,
    users_f,
    pick,
    embedded,
    raw,
    chosen,
    pre_one,
    hidden_one,
    part,
    sends,
    parts_in,
    in_sems,
    load_sems,
    user_send,
    user_recv,
    part_send,
    part_recv,
):
    me = lax.axis_index("items")
    owned = query.shape[0]
    requests = n * owned
    width = embedded.shape[1]
    catalog = embedded.shape[0]
    depth = tower.shape[0]
    per_shard = kept.shape[0]
    hidden = first.shape[1]
    shards = n // 2
    block = requests // 2
    rows = block * per_shard
    upper = me >= shards
    base = [jnp.where(upper, shards, 0), jnp.where(upper, 0, shards)]
    local = me - base[0]

    def turn(i, k):
        return jnp.where(i + k >= shards, i + k - shards, i + k)

    peers = [(shards + k, 1, turn(local, k)) for k in range(shards)]
    peers += [(k, 0, turn(local, k)) for k in range(1, shards)]

    kept_load = pltpu.make_async_copy(kept, kept_v, load_sems.at[1])
    kept_load.start()
    barrier = pltpu.get_barrier_semaphore()
    for slot, side, i in peers:
        pl.semaphore_signal(
            barrier,
            inc=1,
            device_id={"items": base[side] + i},
            device_id_type=pl.DeviceIdType.MESH,
        )

    step = depth // CUTS
    tower_loads = []
    for c in range(CUTS):
        at = pl.ds(c * step, step)
        pair = (
            pltpu.make_async_copy(tower.at[at, :], tower_v.at[at, :], in_sems.at[2 * c]),
            pltpu.make_async_copy(traits.at[:, at], traits_v.at[:, at], in_sems.at[2 * c + 1]),
        )
        for load in pair:
            load.start()
        tower_loads.append(pair)
    own_users = pltpu.make_async_copy(query, users_in.at[me], load_sems.at[0])
    first_load = pltpu.make_async_copy(first, first_v, load_sems.at[2])
    second_load = pltpu.make_async_copy(second, second_v, load_sems.at[3])
    final_load = pltpu.make_async_copy(final, final_v, load_sems.at[4])
    for load in (first_load, second_load, own_users, final_load):
        load.start()

    def user_copy(slot, side, i):
        return pltpu.make_async_remote_copy(
            src_ref=query,
            dst_ref=users_in.at[me],
            send_sem=user_send.at[slot],
            recv_sem=user_recv.at[me],
            device_id={"items": base[side] + i},
            device_id_type=pl.DeviceIdType.MESH,
        )

    def user_arrival(slot, side, i):
        source = base[side] + i
        return pltpu.make_async_remote_copy(
            src_ref=query,
            dst_ref=users_in.at[source],
            send_sem=user_send.at[slot],
            recv_sem=user_recv.at[source],
            device_id={"items": source},
            device_id_type=pl.DeviceIdType.MESH,
        )

    kept_load.wait()
    columns = kept_v[...].T
    places = lax.broadcasted_iota(jnp.int32, (block, catalog), 1)
    for side in range(2):
        low, high = columns[:block], columns[block:]
        mine = jnp.where(upper, high, low) if side == 0 else jnp.where(upper, low, high)
        for j in range(per_shard):
            at = side * rows + j * block
            pick[at : at + block, :] = jnp.where(
                mine[:, j : j + 1] == places, 1.0, 0.0
            ).astype(BF16)

    for c in range(CUTS):
        if c == GREET_AFTER:
            pl.semaphore_wait(barrier, n - 1)
            for peer in peers:
                user_copy(*peer).start()
        for load in tower_loads[c]:
            load.wait()
        at = pl.ds(c * step, step)
        term = jnp.dot(traits_v[:, at], tower_v[at, :], preferred_element_type=F32)
        if c == 0:
            raw[...] = term
        elif c < CUTS - 1:
            raw[...] += term
        else:
            total = raw[...] + term
            factor = lax.rsqrt(jnp.mean(total * total, axis=-1, keepdims=True) + 1e-06)
            embedded[...] = (total * factor).astype(BF16)

    chosen[...] = jnp.dot(pick[...], embedded[...], preferred_element_type=F32).astype(BF16)
    first_load.wait()
    pre_one[...] = jnp.dot(chosen[...], first_v[width:, :], preferred_element_type=F32)
    final_load.wait()
    final_rows = final_v[...].astype(F32)
    final_row = jnp.concatenate(
        [final_rows[i : i + 1, :] for i in range(hidden // LANES)], axis=1
    )
    final_wide = jnp.broadcast_to(final_row, (LANES, hidden)).astype(BF16)
    lane = lax.broadcasted_iota(jnp.int32, (block, LANES), 1)
    shards_per_tile = LANES // per_shard
    home = lax.rem(me, shards_per_tile) * per_shard
    second_load.wait()

    def part_copy(slot, side, i):
        return pltpu.make_async_remote_copy(
            src_ref=sends.at[side, i],
            dst_ref=parts_in.at[me],
            send_sem=part_send.at[slot],
            recv_sem=part_recv.at[me],
            device_id={"items": base[side] + i},
            device_id_type=pl.DeviceIdType.MESH,
        )

    def part_arrival(slot, side, i):
        source = base[side] + i
        return pltpu.make_async_remote_copy(
            src_ref=sends.at[side, i],
            dst_ref=parts_in.at[source],
            send_sem=part_send.at[slot],
            recv_sem=part_recv.at[source],
            device_id={"items": source},
            device_id_type=pl.DeviceIdType.MESH,
        )

    own_users.wait()
    for side in range(2):
        for peer in peers:
            if peer[1] == side:
                user_arrival(*peer).wait_recv()
        for i in range(shards):
            users_f[side, i * owned : (i + 1) * owned, :] = users_in[base[side] + i].astype(F32)
        users = users_f[side].astype(BF16)
        span = slice(side * rows, (side + 1) * rows)
        product = chosen[span, :] * jnp.concatenate([users] * per_shard, axis=0)
        for t in range(hidden // TILE):
            at = slice(t * TILE, (t + 1) * TILE)
            hidden_one[:, at] = silu(
                pre_one[span, at]
                + jnp.dot(product, first_v[:width, at], preferred_element_type=F32)
            ).astype(BF16)
        scores = None
        for t in range(hidden // TILE):
            at = slice(t * TILE, (t + 1) * TILE)
            hidden_two = silu(
                jnp.dot(hidden_one[...], second_v[:, at], preferred_element_type=F32)
            ).astype(BF16)
            term = nt_dot(hidden_two, final_wide[:, at])
            scores = term if scores is None else scores + term
        mine = jnp.zeros((block, LANES), F32)
        for j in range(per_shard):
            mine = jnp.where(
                lane == home + j, scores[j * block : (j + 1) * block, :], mine
            )
        part[...] = mine
        for i in range(shards):
            sends[side, i] = part[i * owned : (i + 1) * owned, :]
        for peer in peers:
            if peer[1] == side:
                part_copy(*peer).start()

    near, far = users_f[0].astype(BF16), users_f[1].astype(BF16)
    scale = width ** (-0.5)
    pre_v[:block, :] = nt_dot(jnp.where(upper, far, near), embedded[...]) * scale
    pre_v[block:, :] = nt_dot(jnp.where(upper, near, far), embedded[...]) * scale

    parts_in[me] = sends[0, local]
    for peer in peers:
        part_arrival(*peer).wait_recv()
    for t in range(n // shards_per_tile):
        total = parts_in[t * shards_per_tile]
        for s in range(t * shards_per_tile + 1, (t + 1) * shards_per_tile):
            total = total + parts_in[s]
        rank_v[:, t * LANES : (t + 1) * LANES] = total
    for peer in peers:
        user_copy(*peer).wait_send()
        part_copy(*peer).wait_send()


def per_device(
    n,
    candidate_traits,
    candidate_tower_matrix,
    query_vectors,
    kept_positions,
    ranker_first_matrix,
    ranker_second_matrix,
    ranker_final_vector,
):
    catalog, depth = candidate_traits.shape
    width = candidate_tower_matrix.shape[1]
    owned = query_vectors.shape[0]
    requests, per_shard = kept_positions.shape
    hidden = ranker_first_matrix.shape[1]
    picked = requests * per_shard
    anywhere = pl.BlockSpec(memory_space=pl.ANY)
    inside = pl.BlockSpec(memory_space=pltpu.VMEM)
    prescore, ranking = pl.pallas_call(
        functools.partial(cascade, n),
        out_shape=(
            pltpu.VMEM((requests, catalog), F32),
            pltpu.VMEM((owned, n * per_shard), F32),
        ),
        in_specs=[anywhere] * 7,
        out_specs=(inside, inside),
        scratch_shapes=[
            pltpu.VMEM((catalog, depth), BF16),
            pltpu.VMEM((depth, width), BF16),
            pltpu.VMEM(ranker_first_matrix.shape, BF16),
            pltpu.VMEM(ranker_second_matrix.shape, BF16),
            pltpu.VMEM((hidden // LANES, LANES), BF16),
            pltpu.VMEM((per_shard, requests), jnp.int32),
            pltpu.VMEM((n, owned, width), BF16),
            pltpu.VMEM((2, requests // 2, width), F32),
            pltpu.VMEM((picked, catalog), BF16),
            pltpu.VMEM((catalog, width), BF16),
            pltpu.VMEM((catalog, width), F32),
            pltpu.VMEM((picked, width), BF16),
            pltpu.VMEM((picked, hidden), F32),
            pltpu.VMEM((picked // 2, hidden), BF16),
            pltpu.VMEM((requests // 2, LANES), F32),
            pltpu.VMEM((2, n // 2, owned, LANES), F32),
            pltpu.VMEM((n, owned, LANES), F32),
            pltpu.SemaphoreType.DMA((2 * CUTS,)),
            pltpu.SemaphoreType.DMA((5,)),
            pltpu.SemaphoreType.DMA((n,)),
            pltpu.SemaphoreType.DMA((n,)),
            pltpu.SemaphoreType.DMA((n,)),
            pltpu.SemaphoreType.DMA((n,)),
        ],
        compiler_params=pltpu.CompilerParams(collective_id=0, has_side_effects=True),
        name="cascade",
    )(
        candidate_traits,
        candidate_tower_matrix,
        query_vectors,
        kept_positions.T,
        ranker_first_matrix,
        ranker_second_matrix,
        ranker_final_vector.reshape(hidden // LANES, LANES),
    )
    return (prescore.T, ranking)


def solution(mesh):
    placed = (
        P(("groups", "items"), None),
        P(),
        P(("groups", "items"), None),
        P("groups", "items"),
        P(),
        P(),
        P(),
    )
    return jax.shard_map(
        functools.partial(per_device, mesh.shape["items"]),
        mesh=mesh,
        in_specs=placed,
        out_specs=(P(("groups", "items"), None), P(("groups", "items"), None)),
        check_vma=False,
    )
```

time: 22.9 us -> 19 us (0.83)
  Pallas kernels: 19.3 us -> 16.9 us
  local copies, waits for them, and re-layouts: 2.83 us -> 1.24 us
    pallas_call x1, Pallas kernels: 19.3 us -> 16.9 us  [per_device(): pl.pallas_call(functools.partial(cascade, n), out_shape=(pltpu.VMEM((requ...]
    unnamed x2, local copies, waits for them, and re-layouts: 2.83 us -> 1.24 us
where the time goes in v2:
time: 19 us; the launch traced here: 18.8 us
  Pallas kernels  16.9 us (89%)
  local copies, waits for them, and re-layouts  1.24 us (7%)
  between operations  0.64 us (3%)
    pallas_call x1, Pallas kernels, per_device(): pl.pallas_call(functools.partial(cascade, n), out_shape=(pltpu.VMEM((requ...  16.9 us
    unnamed x2, local copies, waits for them, and re-layouts  1.24 us

profile of v2, /device:TPU:0, one launch (start us, length us, event | category | flops | bytes accessed | tf_op | source)
XLA Modules:
  0.0 18.8 jit_solution(16441298538719395265)
XLA Ops:
  0.6 16.9 %cascade.1 = (f32[64,512]{1,0:T(8,128)S(1)}, f32[4,128]{1,0:T(4,128)S(1)}) custom-call(bf16[512,2048]{1,0:T(8,128)(2,1)} %traits.1, bf16[2048,512]{1,0:T(8,128)(2,1)} %tower.1, bf16[4,512]{1,0:T(4,128)(2,1)} %query.1, s32[8,64]{1,0:T(8,128)} %bitcast.4, bf16[1024,1024]{1,0:T(8,128)(2,1)} %first.1, bf16[1024,1024]{1,0:T(8,128)(2,1)} %second.1, ...), custom_call_target="tpu_custom_call" | custom-call | tf_op jit(solution)/shard_map/cascade/pallas_call | solution.py:270
  17.6 0.7 %copy.11 = f32[512,64]{0,1:T(8,128)} copy(f32[512,64]{0,1:T(8,128)S(1)} %bitcast.3) | data formatting | bytes 262144
  18.2 0.6 %copy.12 = f32[4,128]{1,0:T(4,128)} copy(f32[4,128]{1,0:T(4,128)S(1)} %get-tuple-element.7) | data formatting | bytes 4096

commit v3 on v2

--- a/solution.py
+++ b/solution.py
@@ -8,15 +8,14 @@
 from jax.sharding import PartitionSpec as P
 
 LANES = 128
-TILE = 256
+TILE = 1024
 CUTS = 4
-GREET_AFTER = 1
+GREET_BEFORE = 1
 F32 = jnp.float32
 BF16 = jnp.bfloat16
 
 
-def silu(v):
-    half = 0.5 * v
+def silu_of_half(half):
     return half + half * jnp.tanh(half)
 
 
@@ -68,20 +67,28 @@
     per_shard = kept.shape[0]
     hidden = first.shape[1]
     shards = n // 2
-    block = requests // 2
-    rows = block * per_shard
+    quarter = n // 4
     upper = me >= shards
-    base = [jnp.where(upper, shards, 0), jnp.where(upper, 0, shards)]
+
+    def either(if_upper, if_lower):
+        return jnp.where(upper, if_upper, if_lower)
+
+    counts = [shards, quarter, quarter]
+    base = [either(shards, 0), either(quarter, shards), either(0, shards + quarter)]
+    starts = [0, shards * owned, (shards + quarter) * owned]
     local = me - base[0]
 
     def turn(i, k):
         return jnp.where(i + k >= shards, i + k - shards, i + k)
 
-    peers = [(shards + k, 1, turn(local, k)) for k in range(shards)]
+    peers = [(shards + quarter + k, 2, k) for k in range(quarter)]
+    peers += [(shards + k, 1, k) for k in range(quarter)]
     peers += [(k, 0, turn(local, k)) for k in range(1, shards)]
 
     kept_load = pltpu.make_async_copy(kept, kept_v, load_sems.at[1])
+    own_users = pltpu.make_async_copy(query, users_in.at[me], load_sems.at[0])
     kept_load.start()
+    own_users.start()
     barrier = pltpu.get_barrier_semaphore()
     for slot, side, i in peers:
         pl.semaphore_signal(
@@ -102,16 +109,15 @@
         for load in pair:
             load.start()
         tower_loads.append(pair)
-    own_users = pltpu.make_async_copy(query, users_in.at[me], load_sems.at[0])
     first_load = pltpu.make_async_copy(first, first_v, load_sems.at[2])
     second_load = pltpu.make_async_copy(second, second_v, load_sems.at[3])
     final_load = pltpu.make_async_copy(final, final_v, load_sems.at[4])
-    for load in (first_load, second_load, own_users, final_load):
+    for load in (first_load, second_load, final_load):
         load.start()
 
     def user_copy(slot, side, i):
         return pltpu.make_async_remote_copy(
-            src_ref=query,
+            src_ref=users_in.at[me],
             dst_ref=users_in.at[me],
             send_sem=user_send.at[slot],
             recv_sem=user_recv.at[me],
@@ -122,7 +128,7 @@
     def user_arrival(slot, side, i):
         source = base[side] + i
         return pltpu.make_async_remote_copy(
-            src_ref=query,
+            src_ref=users_in.at[me],
             dst_ref=users_in.at[source],
             send_sem=user_send.at[slot],
             recv_sem=user_recv.at[source],
@@ -131,19 +137,25 @@
         )
 
     kept_load.wait()
+    own_users.wait()
     columns = kept_v[...].T
-    places = lax.broadcasted_iota(jnp.int32, (block, catalog), 1)
-    for side in range(2):
-        low, high = columns[:block], columns[block:]
-        mine = jnp.where(upper, high, low) if side == 0 else jnp.where(upper, low, high)
+    part_of = [columns[q * quarter * owned : (q + 1) * quarter * owned] for q in range(4)]
+    columns_of = [
+        either(jnp.concatenate(part_of[2:]), jnp.concatenate(part_of[:2])),
+        either(part_of[1], part_of[2]),
+        either(part_of[0], part_of[3]),
+    ]
+    for side in range(3):
+        block = counts[side] * owned
+        places = lax.broadcasted_iota(jnp.int32, (block, catalog), 1)
         for j in range(per_shard):
-            at = side * rows + j * block
+            at = starts[side] * per_shard + j * block
             pick[at : at + block, :] = jnp.where(
-                mine[:, j : j + 1] == places, 1.0, 0.0
+                columns_of[side][:, j : j + 1] == places, 0.5, 0.0
             ).astype(BF16)
 
     for c in range(CUTS):
-        if c == GREET_AFTER:
+        if c == GREET_BEFORE:
             pl.semaphore_wait(barrier, n - 1)
             for peer in peers:
                 user_copy(*peer).start()
@@ -169,14 +181,13 @@
         [final_rows[i : i + 1, :] for i in range(hidden // LANES)], axis=1
     )
     final_wide = jnp.broadcast_to(final_row, (LANES, hidden)).astype(BF16)
-    lane = lax.broadcasted_iota(jnp.int32, (block, LANES), 1)
     shards_per_tile = LANES // per_shard
     home = lax.rem(me, shards_per_tile) * per_shard
     second_load.wait()
 
     def part_copy(slot, side, i):
         return pltpu.make_async_remote_copy(
-            src_ref=sends.at[side, i],
+            src_ref=sends.at[base[side] + i],
             dst_ref=parts_in.at[me],
             send_sem=part_send.at[slot],
             recv_sem=part_recv.at[me],
@@ -187,7 +198,7 @@
     def part_arrival(slot, side, i):
         source = base[side] + i
         return pltpu.make_async_remote_copy(
-            src_ref=sends.at[side, i],
+            src_ref=sends.at[source],
             dst_ref=parts_in.at[source],
             send_sem=part_send.at[slot],
             recv_sem=part_recv.at[source],
@@ -195,48 +206,54 @@
             device_id_type=pl.DeviceIdType.MESH,
         )
 
-    own_users.wait()
-    for side in range(2):
+    for side in range(3):
+        block = counts[side] * owned
         for peer in peers:
             if peer[1] == side:
                 user_arrival(*peer).wait_recv()
-        for i in range(shards):
-            users_f[side, i * owned : (i + 1) * owned, :] = users_in[base[side] + i].astype(F32)
-        users = users_f[side].astype(BF16)
-        span = slice(side * rows, (side + 1) * rows)
+        for i in range(counts[side]):
+            at = starts[side] + i * owned
+            users_f[at : at + owned, :] = users_in[base[side] + i].astype(F32)
+        users = users_f[starts[side] : starts[side] + block, :].astype(BF16)
+        span = slice(starts[side] * per_shard, (starts[side] + block) * per_shard)
+        own = slice(0, block * per_shard)
         product = chosen[span, :] * jnp.concatenate([users] * per_shard, axis=0)
         for t in range(hidden // TILE):
             at = slice(t * TILE, (t + 1) * TILE)
-            hidden_one[:, at] = silu(
-                pre_one[span, at]
-                + jnp.dot(product, first_v[:width, at], preferred_element_type=F32)
-            ).astype(BF16)
+            half = pre_one[span, at] + jnp.dot(
+                product, first_v[:width, at], preferred_element_type=F32
+            )
+            hidden_one[own, at] = silu_of_half(half).astype(BF16) * jnp.asarray(0.5, BF16)
         scores = None
         for t in range(hidden // TILE):
             at = slice(t * TILE, (t + 1) * TILE)
-            hidden_two = silu(
-                jnp.dot(hidden_one[...], second_v[:, at], preferred_element_type=F32)
-            ).astype(BF16)
-            term = nt_dot(hidden_two, final_wide[:, at])
+            half = jnp.dot(hidden_one[own, :], second_v[:, at], preferred_element_type=F32)
+            term = nt_dot(silu_of_half(half).astype(BF16), final_wide[:, at])
             scores = term if scores is None else scores + term
+        lane = lax.broadcasted_iota(jnp.int32, (block, LANES), 1)
         mine = jnp.zeros((block, LANES), F32)
         for j in range(per_shard):
             mine = jnp.where(
                 lane == home + j, scores[j * block : (j + 1) * block, :], mine
             )
-        part[...] = mine
-        for i in range(shards):
-            sends[side, i] = part[i * owned : (i + 1) * owned, :]
+        part[:block, :] = mine
+        for i in range(counts[side]):
+            sends[base[side] + i] = part[i * owned : (i + 1) * owned, :]
         for peer in peers:
             if peer[1] == side:
                 part_copy(*peer).start()
 
-    near, far = users_f[0].astype(BF16), users_f[1].astype(BF16)
-    scale = width ** (-0.5)
-    pre_v[:block, :] = nt_dot(jnp.where(upper, far, near), embedded[...]) * scale
-    pre_v[block:, :] = nt_dot(jnp.where(upper, near, far), embedded[...]) * scale
-
-    parts_in[me] = sends[0, local]
+    near, mid = users_f[: starts[1], :], users_f[starts[1] : starts[2], :]
+    far = users_f[starts[2] :, :]
+    ordered = either(
+        jnp.concatenate([far, mid, near]), jnp.concatenate([near, mid, far])
+    ).astype(BF16)
+    pre_v[...] = nt_dot(ordered, embedded[...]) * width ** (-0.5)
+
+    parts_in[me] = sends[me]
+    for peer in peers:
+        user_copy(*peer).wait_send()
+        part_copy(*peer).wait_send()
     for peer in peers:
         part_arrival(*peer).wait_recv()
     for t in range(n // shards_per_tile):
@@ -244,9 +261,6 @@
         for s in range(t * shards_per_tile + 1, (t + 1) * shards_per_tile):
             total = total + parts_in[s]
         rank_v[:, t * LANES : (t + 1) * LANES] = total
-    for peer in peers:
-        user_copy(*peer).wait_send()
-        part_copy(*peer).wait_send()
 
 
 def per_device(
@@ -283,7 +297,7 @@
             pltpu.VMEM((hidden // LANES, LANES), BF16),
             pltpu.VMEM((per_shard, requests), jnp.int32),
             pltpu.VMEM((n, owned, width), BF16),
-            pltpu.VMEM((2, requests // 2, width), F32),
+            pltpu.VMEM((requests, width), F32),
             pltpu.VMEM((picked, catalog), BF16),
             pltpu.VMEM((catalog, width), BF16),
             pltpu.VMEM((catalog, width), F32),
@@ -291,7 +305,7 @@
             pltpu.VMEM((picked, hidden), F32),
             pltpu.VMEM((picked // 2, hidden), BF16),
             pltpu.VMEM((requests // 2, LANES), F32),
-            pltpu.VMEM((2, n // 2, owned, LANES), F32),
+            pltpu.VMEM((n, owned, LANES), F32),
             pltpu.VMEM((n, owned, LANES), F32),
             pltpu.SemaphoreType.DMA((2 * CUTS,)),
             pltpu.SemaphoreType.DMA((5,)),

time: 19 us -> 18.1 us (0.953)
  Pallas kernels: 16.9 us -> 16.1 us
    pallas_call x1, Pallas kernels: 16.9 us -> 16.1 us  [per_device(): pl.pallas_call(functools.partial(cascade, n), out_shape=(pltpu.VMEM((requ...]
where the time goes in v3:
time: 18.1 us; the launch traced here: 17.9 us
  Pallas kernels  16.1 us (89%)
  local copies, waits for them, and re-layouts  1.24 us (7%)
  between operations  0.64 us (4%)
    pallas_call x1, Pallas kernels, per_device(): pl.pallas_call(functools.partial(cascade, n), out_shape=(pltpu.VMEM((requ...  16.1 us
    unnamed x2, local copies, waits for them, and re-layouts  1.24 us

profile of v3, /device:TPU:0, one launch (start us, length us, event | category | flops | bytes accessed | tf_op | source)
XLA Modules:
  0.0 17.9 jit_solution(284838311799778315)
XLA Ops:
  0.6 16.1 %cascade.1 = (f32[64,512]{1,0:T(8,128)S(1)}, f32[4,128]{1,0:T(4,128)S(1)}) custom-call(bf16[512,2048]{1,0:T(8,128)(2,1)} %traits.1, bf16[2048,512]{1,0:T(8,128)(2,1)} %tower.1, bf16[4,512]{1,0:T(4,128)(2,1)} %query.1, s32[8,64]{1,0:T(8,128)} %bitcast.4, bf16[1024,1024]{1,0:T(8,128)(2,1)} %first.1, bf16[1024,1024]{1,0:T(8,128)(2,1)} %second.1, ...), custom_call_target="tpu_custom_call" | custom-call | tf_op jit(solution)/shard_map/cascade/pallas_call | solution.py:284
  16.7 0.7 %copy.11 = f32[512,64]{0,1:T(8,128)} copy(f32[512,64]{0,1:T(8,128)S(1)} %bitcast.3) | data formatting | bytes 262144
  17.4 0.6 %copy.12 = f32[4,128]{1,0:T(4,128)} copy(f32[4,128]{1,0:T(4,128)S(1)} %get-tuple-element.7) | data formatting | bytes 4096

commit v4 on v3

--- a/solution.py
+++ b/solution.py
@@ -180,7 +180,6 @@
     final_row = jnp.concatenate(
         [final_rows[i : i + 1, :] for i in range(hidden // LANES)], axis=1
     )
-    final_wide = jnp.broadcast_to(final_row, (LANES, hidden)).astype(BF16)
     shards_per_tile = LANES // per_shard
     home = lax.rem(me, shards_per_tile) * per_shard
     second_load.wait()
@@ -228,7 +227,8 @@
         for t in range(hidden // TILE):
             at = slice(t * TILE, (t + 1) * TILE)
             half = jnp.dot(hidden_one[own, :], second_v[:, at], preferred_element_type=F32)
-            term = nt_dot(silu_of_half(half).astype(BF16), final_wide[:, at])
+            hidden_two = silu_of_half(half).astype(BF16).astype(F32)
+            term = jnp.sum(hidden_two * final_row[:, at], axis=1, keepdims=True)
             scores = term if scores is None else scores + term
         lane = lax.broadcasted_iota(jnp.int32, (block, LANES), 1)
         mine = jnp.zeros((block, LANES), F32)

time: 18.1 us -> 17.8 us (0.983)
  Pallas kernels: 16.1 us -> 15.7 us
    pallas_call x1, Pallas kernels: 16.1 us -> 15.7 us  [per_device(): pl.pallas_call(functools.partial(cascade, n), out_shape=(pltpu.VMEM((requ...]
where the time goes in v4:
time: 17.8 us; the launch traced here: 17.6 us
  Pallas kernels  15.7 us (88%)
  local copies, waits for them, and re-layouts  1.24 us (7%)
  between operations  0.64 us (4%)
    pallas_call x1, Pallas kernels, per_device(): pl.pallas_call(functools.partial(cascade, n), out_shape=(pltpu.VMEM((requ...  15.7 us
    unnamed x2, local copies, waits for them, and re-layouts  1.24 us

profile of v4, /device:TPU:0, one launch (start us, length us, event | category | flops | bytes accessed | tf_op | source)
XLA Modules:
  0.0 17.6 jit_solution(16008992574422406815)
XLA Ops:
  0.6 15.7 %cascade.1 = (f32[64,512]{1,0:T(8,128)S(1)}, f32[4,128]{1,0:T(4,128)S(1)}) custom-call(bf16[512,2048]{1,0:T(8,128)(2,1)} %traits.1, bf16[2048,512]{1,0:T(8,128)(2,1)} %tower.1, bf16[4,512]{1,0:T(4,128)(2,1)} %query.1, s32[8,64]{1,0:T(8,128)} %bitcast.4, bf16[1024,1024]{1,0:T(8,128)(2,1)} %first.1, bf16[1024,1024]{1,0:T(8,128)(2,1)} %second.1, ...), custom_call_target="tpu_custom_call" | custom-call | tf_op jit(solution)/shard_map/cascade/pallas_call | solution.py:284
  16.4 0.7 %copy.11 = f32[512,64]{0,1:T(8,128)} copy(f32[512,64]{0,1:T(8,128)S(1)} %bitcast.3) | data formatting | bytes 262144
  17.0 0.6 %copy.12 = f32[4,128]{1,0:T(4,128)} copy(f32[4,128]{1,0:T(4,128)S(1)} %get-tuple-element.7) | data formatting | bytes 4096
